TPU v7x, 128 devices: a whole 4x4x4 slice. The times are simulated.
128 devices in a mesh: tm: 64 (over z_hi, x, y, core), inp: 2 (over z_lo).
Axes of the slice: x: 4, y: 4, z: 4 (z_hi: 2, z_lo: 2; z = z_hi * 2 + z_lo), core: 2. Of those that a mesh axis runs over, the one named last changes fastest.
Arguments:
- voltages: bfloat16 [2, 262144, 1024], P(None, 'tm', 'inp'), may hold values from -127 to 127, as said below
- taps: int32 [12, 1024], replicated, may hold values from -64 to 64
Outputs:
- visibility: bfloat16 [512, 1024, 1024], P(('tm', 'inp'))
Inputs may be any that keep to these rules, and one draw needn't show every extreme that they name: `voltages`: every sample is a whole number.
All inputs are finite; a program needn't handle non-finite values.
Results may differ from a plain program's by a relative error of at most 0.0048.
Values may be sent and summed in bfloat16 or wider, within the bound.
A program may use at most 576 MiB of HBM per device.

v0:
```python
import math
import jax
import jax.numpy as jnp
from jax import lax
from jax.sharding import PartitionSpec as P

KEEP = 512


def passed_along(value, axis, steps):
    count = lax.axis_size(axis)
    first, last = (max(0, -steps), min(count, count - steps))
    return lax.ppermute(value, axis, [(source, source + steps) for source in range(first, last)])


def dft_table(fine_count, keep_count):
    branch = jnp.arange(fine_count, dtype=jnp.int32)[:, None]
    channel = jnp.arange(keep_count, dtype=jnp.int32)[None, :] - keep_count // 2
    phase_index = jnp.mod(branch * channel, fine_count).astype(jnp.float32)
    angles = 2.0 * math.pi / fine_count * phase_index
    norm_scale = 1.0 / math.sqrt(fine_count)
    cosine = jnp.cos(angles) * norm_scale
    sine_part = jnp.sin(angles) * norm_scale
    dft_matrix = jnp.stack(
        [jnp.stack([cosine, -sine_part], 1), jnp.stack([sine_part, cosine], 1)], 0
    )
    return dft_matrix.astype(jnp.bfloat16)


def finish(products, chan_count, all_inputs, spec_total):
    visibility = products.reshape(chan_count, 2, all_inputs, all_inputs) * (1.0 / spec_total)
    upper_mask = jnp.arange(all_inputs)[:, None] <= jnp.arange(all_inputs)[None, :]
    return jnp.where(upper_mask[None], visibility[:, 0], visibility[:, 1]).astype(jnp.bfloat16)


def per_device(voltages, taps):
    history_len = taps.shape[0] - 1
    fine_count = taps.shape[1]
    frames = voltages.shape[1] // fine_count
    input_width = voltages.shape[2]
    keep_count = KEEP
    coefficient = taps.astype(jnp.float32)
    dft_matrix = dft_table(fine_count, keep_count)
    n_time = lax.axis_size("tm")
    n_group = lax.axis_size("inp")
    chan_count = keep_count // (n_time * n_group)
    all_inputs = n_group * input_width
    spec_total = n_time * frames
    own_frames = voltages.reshape(2, frames, fine_count, input_width)
    pieces = [own_frames]
    remaining = history_len
    shift_count = (history_len + frames - 1) // frames
    for offset in range(1, shift_count + 1):
        take_count = min(remaining, frames)
        received = passed_along(own_frames[:, frames - take_count :], "tm", offset)
        pieces.insert(0, received)
        remaining = remaining - take_count
    extended = jnp.concatenate(pieces, axis=1)
    filtered = coefficient[0][None, None, :, None] * extended[
        :, history_len : history_len + frames
    ].astype(jnp.float32)
    for k in range(1, history_len + 1):
        filtered = filtered + coefficient[k][None, None, :, None] * extended[
            :, history_len - k : history_len - k + frames
        ].astype(jnp.float32)
    filtered = (filtered * (1.0 / 8192.0)).astype(jnp.bfloat16)
    spectra = jnp.einsum(
        "rfna,rnsj->jsfa", filtered, dft_matrix, preferred_element_type=jnp.float32
    ).astype(jnp.bfloat16)
    flat_spectra = spectra.reshape(keep_count, 2, frames * input_width)
    exchanged = lax.all_to_all(flat_spectra, ("tm", "inp"), split_axis=0, concat_axis=2, tiled=True)
    channel_grid = exchanged.reshape(chan_count, 2, n_time, n_group, frames, input_width)
    einsum_form = "crtgfa,csrthfb->csgahb"
    rotated = jnp.stack([-channel_grid[:, 1], channel_grid[:, 0]], axis=1)
    turned = jnp.stack([channel_grid, rotated], axis=1)
    products = jnp.einsum(einsum_form, channel_grid, turned, preferred_element_type=jnp.float32)
    return finish(products, chan_count, all_inputs, spec_total)


def solution(mesh):
    placed = (P(None, "tm", "inp"), P())
    return jax.shard_map(
        per_device,
        mesh=mesh,
        in_specs=placed,
        out_specs=P(("tm", "inp"), None, None),
        check_vma=False,
    )
```

profile of v0, /device:TPU:1, one launch (start us, length us, event | category | flops | bytes accessed | tf_op | source)
XLA Modules:
  0.0 758.6 jit_solution(5823844590932739800)
XLA Ops:
  0.0 11.4 %copy.11 = bf16[2,4,1024,512]{2,3,0,1:T(8,128)(2,1)} copy(bf16[2,4,1024,512]{3,2,1,0:T(8,128)(2,1)} %bitcast.81) | data formatting | bytes 16777216 | tf_op jit(solution)/shard_map/reshape | solution.py:49
  11.4 4.7 collective-permute-start.1
  16.0 3.5 collective-permute-start
  19.6 6.8 slice.130
  26.4 5.9 collective-permute-start.2
  32.3 8.8 %negate_convert_fusion = (bf16[1024,1,512]{2,0,1:T(8,128)(2,1)S(1)}, bf16[1024,1,512]{2,0,1:T(8,128)(2,1)S(1)}, bf16[1024,1,512]{2,0,1:T(8,128)(2,1)S(1)}) fusion(s32[512]{0:T(512)S(1)} %iota_add_fusion), kind=kLoop, calls=%fused_computation.35 | loop fusion | flops 10485760 | bytes 3147776 | tf_op jit(solution)/shard_map/convert.7
  42.9 377.9 %collective-permute-done.2 = bf16[2,3,1024,512]{2,3,0,1:T(8,128)(2,1)} collective-permute-done((bf16[2,3,1024,512]{2,3,0,1:T(8,128)(2,1)}, bf16[2,3,1024,512]{2,3,0,1:T(8,128)(2,1)}, u32[]{:S(2)}, u32[]{:S(2)}) %collective-permute-start.2) | collective-permute-done | bytes 6291488 | tf_op jit(solution)/shard_map/ppermute | solution.py:13
  420.8 6.8 constant_dynamic-update-slice_fusion.3
  427.6 7.4 constant_dynamic-update-slice_fusion.1
  436.0 3.3 copy-done.2
  439.3 7.6 %constant_dynamic-update-slice_fusion = bf16[2,8,1024,512]{2,3,0,1:T(8,128)(2,1)} fusion(bf16[2,8,1024,512]{2,3,0,1:T(8,128)(2,1)} %get-tuple-element.5, bf16[2,4,1024,512]{2,3,0,1:T(8,128)(2,1)} %copy-done.2), kind=kLoop, calls=%fused_computation.42 | loop fusion | bytes 16777216 | tf_op jit(solution)/shard_map/concatenate | solution.py:58
  446.9 38.9 %bitcast_convert_fusion = bf16[2,512,4,512]{1,3,2,0:T(8,128)(2,1)} fusion(bf16[2,7,1024,512]{2,3,0,1:T(8,128)(2,1)} %get-tuple-element.6, f32[1024]{0:T(1024)S(1)} %bitcast.84, f32[1024]{0:T(1024)S(1)} %bitcast.85, f32[1024]{0:T(1024)S(1)} %bitcast.86, bf16[2,4,1024,512]{2,3,0,1:T(8,128)(2,1)} %copy-done.1, f32[1024]{0:T(1024)S(1)} %bitcast.87, ...), kind=kOutput, calls=%fused_computation.17 | convolution fusion | flops 8793358336 | bytes 83935232 | tf_op jit(solution)/shard_map/rfna,rnsj->jsfa/dot_general | solution.py:67
  485.8 11.3 %copy.16 = bf16[512,2,2048]{2,1,0:T(2,128)(2,1)} copy(bf16[512,2,2048]{0,2,1:T(8,128)(2,1)} %bitcast.82) | data formatting | bytes 8388608 | tf_op jit(solution)/shard_map/reshape | solution.py:70
  497.1 80.0 %all-to-all-start = ((bf16[512,2,2048]{2,1,0:T(2,128)(2,1)}), bf16[512,2,2048]{2,1,0:T(2,128)(2,1)}, u32[]{:S(2)}, u32[]{:S(2)}) async-start(bf16[512,2,2048]{2,1,0:T(2,128)(2,1)} %copy.16), calls=%async_computation | async-start | bytes 8388608 | tf_op jit(solution)/shard_map/all_to_all | solution.py:71
  577.3 53.5 %all-to-all-done = bf16[512,2,2048]{2,1,0:T(2,128)(2,1)} async-done(((bf16[512,2,2048]{2,1,0:T(2,128)(2,1)}), bf16[512,2,2048]{2,1,0:T(2,128)(2,1)}, u32[]{:S(2)}, u32[]{:S(2)}) %all-to-all-start) | async-done | bytes 4194336 | tf_op jit(solution)/shard_map/all_to_all | solution.py:71
  630.8 7.6 reshape.176
  638.4 7.6 %reshape.175 = bf16[4,1,2,64,2,4,512]{6,5,2,0,4,3,1:T(4,128)(2,1)} reshape(bf16[4,2,128,2048]{3,1,0,2:T(2,128)(2,1)} %bitcast.24) | data formatting | bytes 8388608 | tf_op jit(solution)/shard_map/stack;reshape | solution.py:75
  646.0 3.7 fusion.24
  650.9 2.4 copy_negate_fusion
  653.4 4.4 copy.21
  660.1 20.4 %fusion = bf16[4,2,2,512,2,512]{3,5,2,4,1,0:T(8,128)(2,1)} fusion(bf16[4,1,2,64,2,4,512]{6,3,2,5,4,1,0:T(8,128)(2,1)} %maximum_bitcast_fusion.4, bf16[4,1,2,64,2,4,512]{6,3,2,5,4,1,0:T(8,128)(2,1)} %copy.21, bf16[4,2,64,2,4,512,1,1]{5,4,1,0,3,2,7,6:T(4,128)(2,1)} %bitcast.80), kind=kOutput, calls=%fused_computation.1 | convolution fusion | flops 8623489024 | bytes 29360128 | tf_op jit(solution)/shard_map/crtgfa,csrthfb->csgahb/dot_general | solution.py:76
  680.5 41.5 %copy.23 = bf16[4,2,2,512,2,512]{5,4,3,2,1,0:T(2,128)(2,1)} copy(bf16[4,2,2,512,2,512]{3,5,2,4,1,0:T(8,128)(2,1)} %fusion) | data formatting | bytes 33554432 | tf_op jit(solution)/shard_map/mul | solution.py:31
  722.0 27.3 %mul.287 = bf16[4,2,1024,1024]{3,2,1,0:T(8,128)(2,1)} reshape(bf16[4,2,2,512,2,512]{5,4,3,2,1,0:T(2,128)(2,1)} %copy.23) | data formatting | bytes 33554432 | tf_op jit(solution)/shard_map/mul | solution.py:31
  749.3 9.3 %fusion.2 = bf16[4,1024,1024]{2,1,0:T(8,128)(2,1)} fusion(bf16[4,2,1024,1024]{3,2,1,0:T(8,128)(2,1)} %mul.287, pred[1024,1024]{1,0:T(8,128)(4,1)S(1)} %iota_compare_fusion), kind=kLoop, calls=%fused_computation.8 | loop fusion | flops 4194304 | bytes 26214400 | tf_op jit(solution)/shard_map/convert_element_type | solution.py:33
  (16 shorter events, 6.5 us)
Async XLA Ops:
  11.4 20.9 %copy-start.3 = (s32[12,1024]{1,0:T(8,128)S(1)}, s32[12,1024]{1,0:T(8,128)}, u32[]{:S(2)}) copy-start(s32[12,1024]{1,0:T(8,128)} %param.3) | copy-start | bytes 147460
  11.4 416.3 %collective-permute-start.1 = (bf16[2,4,1024,512]{2,3,0,1:T(8,128)(2,1)}, bf16[2,4,1024,512]{2,3,0,1:T(8,128)(2,1)S(1)}, u32[]{:S(2)}, u32[]{:S(2)}) collective-permute-start(bf16[2,4,1024,512]{2,3,0,1:T(8,128)(2,1)} %copy.11), channel_id=1, source_target_pairs={{0,4},{2,6},{4,8},{6,10},{8,12},{10,14},{12,16},{14,18},{16,20},{1... | collective-permute-start | bytes 25165832 | tf_op jit(solution)/shard_map/ppermute | solution.py:13
  16.0 420.0 %collective-permute-start = (bf16[2,4,1024,512]{2,3,0,1:T(8,128)(2,1)}, bf16[2,4,1024,512]{2,3,0,1:T(8,128)(2,1)S(1)}, u32[]{:S(2)}, u32[]{:S(2)}) collective-permute-start(bf16[2,4,1024,512]{2,3,0,1:T(8,128)(2,1)} %copy.11), channel_id=1, source_target_pairs={{0,2},{2,4},{4,6},{6,8},{8,10},{10,12},{12,14},{14,16},{16,18},{18... | collective-permute-start | bytes 25165832 | tf_op jit(solution)/shard_map/ppermute | solution.py:13
  26.4 394.4 %collective-permute-start.2 = (bf16[2,3,1024,512]{2,3,0,1:T(8,128)(2,1)}, bf16[2,3,1024,512]{2,3,0,1:T(8,128)(2,1)}, u32[]{:S(2)}, u32[]{:S(2)}) collective-permute-start(bf16[2,3,1024,512]{2,3,0,1:T(8,128)(2,1)} %slice.130), channel_id=1, source_target_pairs={{0,6},{2,8},{4,10},{6,12},{8,14},{10,16},{12,18},{14,20},{16,22},{... | collective-permute-start | bytes 18874376 | tf_op jit(solution)/shard_map/ppermute | solution.py:13
  427.6 8.3 %copy-start.1 = (bf16[2,4,1024,512]{2,3,0,1:T(8,128)(2,1)}, bf16[2,4,1024,512]{2,3,0,1:T(8,128)(2,1)S(1)}, u32[]{:S(2)}) copy-start(bf16[2,4,1024,512]{2,3,0,1:T(8,128)(2,1)S(1)} %collective-permute-done.1) | copy-start | bytes 25165828
  436.0 3.3 copy-start.2
  497.1 133.7 %all-to-all-start = ((bf16[512,2,2048]{2,1,0:T(2,128)(2,1)}), bf16[512,2,2048]{2,1,0:T(2,128)(2,1)}, u32[]{:S(2)}, u32[]{:S(2)}) async-start(bf16[512,2,2048]{2,1,0:T(2,128)(2,1)} %copy.16), calls=%async_computation | async-start | bytes 8388608 | tf_op jit(solution)/shard_map/all_to_all | solution.py:71
  646.0 7.4 copy-start
where the time goes:
time: 762 us; the launch traced here: 759 us
  waiting for transfers between devices  431 us (57%)
  local copies, waits for them, and re-layouts  149 us (20%)
  starting transfers between devices  94 us (12%)
  matrix products  59.3 us (8%)
  other arithmetic  24.9 us (3%)
    ppermute x3, waiting for transfers between devices, passed_along(): lax.ppermute(value, axis, [(source, source + steps) for source in range(f...  378 us
    all_to_all x1, starting transfers between devices, per_device(): lax.all_to_all(flat_spectra, ('tm', 'inp'), split_axis=0, concat_axis=2,...  80 us
    mul x2, local copies, waits for them, and re-layouts, finish(): products.reshape(chan_count, 2, all_inputs, all_inputs) * (1.0 / spec_total)  68.8 us
    all_to_all x1, waiting for transfers between devices, per_device(): lax.all_to_all(flat_spectra, ('tm', 'inp'), split_axis=0, concat_axis=2,...  53.5 us
    dot_general x1, matrix products, per_device(): jnp.einsum('rfna,rnsj->jsfa', filtered, dft_matrix, preferred_element_typ...  38.9 us
    dot_general x1, matrix products, per_device(): jnp.einsum(einsum_form, channel_grid, turned, preferred_element_type=jnp....  20.4 us
    unnamed x11, local copies, waits for them, and re-layouts  19.7 us
  transfers between devices with their start and end apart: 4, of which 2 were waited for; matrix products, arithmetic and copies ran while one was open for 4% of the time, Pallas kernels for 0%

commit v1 on v0

--- a/solution.py
+++ b/solution.py
@@ -5,6 +5,14 @@
 from jax.sharding import PartitionSpec as P
 
 KEEP = 512
+
+
+def process_views(frame, chip_axis):
+    state_now = jnp.split(frame, jax.lax.axis_size(chip_axis), axis=0)
+    value_now = jnp.stack(state_now)
+    return jnp.concatenate(
+        jax.lax.all_to_all(value_now, concat_axis=0, split_axis=0, axis_name=chip_axis), axis=2
+    )
 
 
 def passed_along(value, axis, steps):
@@ -68,7 +76,7 @@
         "rfna,rnsj->jsfa", filtered, dft_matrix, preferred_element_type=jnp.float32
     ).astype(jnp.bfloat16)
     flat_spectra = spectra.reshape(keep_count, 2, frames * input_width)
-    exchanged = lax.all_to_all(flat_spectra, ("tm", "inp"), split_axis=0, concat_axis=2, tiled=True)
+    exchanged = process_views(flat_spectra, ("tm", "inp"))
     channel_grid = exchanged.reshape(chan_count, 2, n_time, n_group, frames, input_width)
     einsum_form = "crtgfa,csrthfb->csgahb"
     rotated = jnp.stack([-channel_grid[:, 1], channel_grid[:, 0]], axis=1)

time: 762 us -> 1050 us (1.38); the launches traced: 759 us -> 1030 us
  local copies, waits for them, and re-layouts: 149 us -> 403 us
  other arithmetic: 24.9 us -> 61.1 us
  matrix products: 59.3 us -> 32.4 us
    another operation x0 -> x130, local copies, waits for them, and re-layouts: none -> 117 us  [the longest x129 109 us: process_views(): value_now = jnp.stack(state_now)]
    unnamed x11 -> x255, local copies, waits for them, and re-layouts: 19.7 us -> 107 us
    split x0 -> x135, local copies, waits for them, and re-layouts: none -> 75.7 us  [process_views(): state_now = jnp.split(frame, jax.lax.axis_size(chip_axis), axis=0)]
    dot_general x0 -> x1, other arithmetic: none -> 37.1 us  [per_device(): jnp.einsum('rfna,rnsj->jsfa', filtered, dft_matrix, preferred_element_typ...]
    dot_general x1, matrix products: 38.9 us -> 11.7 us  [per_device(): jnp.einsum('rfna,rnsj->jsfa', filtered, dft_matrix, preferred_element_typ...]
    reshape x2 -> x0, local copies, waits for them, and re-layouts: 18.9 us -> none  [the longest x1 11.3 us: per_device(): flat_spectra = spectra.reshape(keep_count, 2, frames * input_width)]
  transfers between devices with their start and end apart: 4 -> 4, of which waited for: 2 -> 2; matrix products, arithmetic and copies ran while one was open for 4% -> 2% of each run, Pallas kernels for 0% -> 0%
where the time goes in v1:
time: 1050 us; the launch traced here: 1030 us
  waiting for transfers between devices  436 us (42%)
  local copies, waits for them, and re-layouts  403 us (38%)
  starting transfers between devices  94.2 us (9%)
  other arithmetic  61.1 us (6%)
  matrix products  32.4 us (3%)
    ppermute x3, waiting for transfers between devices, passed_along(): lax.ppermute(value, axis, [(source, source + steps) for source in range(f...  382 us
    another operation x129, local copies, waits for them, and re-layouts, process_views(): value_now = jnp.stack(state_now)  109 us
    unnamed x255, local copies, waits for them, and re-layouts  107 us
    all_to_all x1, starting transfers between devices, process_views(): jax.lax.all_to_all(value_now, concat_axis=0, split_axis=0, axis_name=chip...  80.1 us
    split x135, local copies, waits for them, and re-layouts, process_views(): state_now = jnp.split(frame, jax.lax.axis_size(chip_axis), axis=0)  75.7 us
    mul x2, local copies, waits for them, and re-layouts, finish(): products.reshape(chan_count, 2, all_inputs, all_inputs) * (1.0 / spec_total)  68.9 us
    all_to_all x1, waiting for transfers between devices, process_views(): jax.lax.all_to_all(value_now, concat_axis=0, split_axis=0, axis_name=chip...  53.5 us
    dot_general x1, other arithmetic, per_device(): jnp.einsum('rfna,rnsj->jsfa', filtered, dft_matrix, preferred_element_typ...  37.1 us
  transfers between devices with their start and end apart: 4, of which 2 were waited for; matrix products, arithmetic and copies ran while one was open for 2% of the time, Pallas kernels for 0%

profile of v1, /device:TPU:1, one launch (start us, length us, event | category | flops | bytes accessed | tf_op | source)
XLA Modules:
  0.0 1026.8 jit_solution(16448535983829707335)
XLA Ops:
  0.0 7.3 copy.11
  7.3 7.4 collective-permute-start.1
  16.6 3.6 slice.257
  20.2 4.8 collective-permute-start.2
  25.0 9.2 negate_convert_fusion
  34.6 382.1 %collective-permute-done.2 = bf16[2,3,1024,512]{3,2,0,1:T(8,128)(2,1)} collective-permute-done((bf16[2,3,1024,512]{3,2,0,1:T(8,128)(2,1)S(1)}, bf16[2,3,1024,512]{3,2,0,1:T(8,128)(2,1)}, u32[]{:S(2)}, u32[]{:S(2)}) %collective-permute-start.2) | collective-permute-done | bytes 6291488 | tf_op jit(solution)/shard_map/ppermute | solution.py:21
  416.7 3.6 constant_dynamic-update-slice_fusion.5
  420.3 7.5 constant_dynamic-update-slice_fusion.3
  427.8 12.4 %constant_dynamic-update-slice_fusion.1 = (bf16[2,8,1024,512]{3,2,0,1:T(8,128)(2,1)}, bf16[2,8,1024,512]{3,2,0,1:T(8,128)(2,1)}) fusion(bf16[2,4,1024,512]{3,2,0,1:T(8,128)(2,1)} %collective-permute-done, bf16[2,8,1024,512]{3,2,0,1:T(8,128)(2,1)} %get-tuple-element.7), kind=kLoop, calls=%fused_computation.37 | loop fusion | bytes 25165824
  440.9 7.2 constant_dynamic-update-slice_fusion
  448.0 37.1 %fusion.36 = bf16[2,4,1024,512,1]{3,2,0,1,4:T(8,128)(2,1)} fusion(bf16[2,7,1024,512]{3,2,0,1:T(8,128)(2,1)} %copy-done, f32[1024]{0:T(1024)S(1)} %bitcast.88, f32[1024]{0:T(1024)S(1)} %bitcast.89, f32[1024]{0:T(1024)S(1)} %bitcast.90, bf16[2,4,1024,512]{3,2,0,1:T(8,128)(2,1)} %collective-permute-done.1, f32[1024]{0:T(1024)S(1)} %bitcast.91, ...), kind=kLoop, calls=%fused_computation.12.clone.clone.clone.2 | loop fusion | flops 155189248 | bytes 109101056 | tf_op jit(solution)/shard_map/rfna,rnsj->jsfa/dot_general | solution.py:75
  485.2 11.7 %fusion.7 = bf16[512,2,4,512]{3,0,2,1:T(8,128)(2,1)S(1)} fusion(bf16[1,1024,2,512]{1,3,0,2:T(8,128)(2,1)S(1)} %get-tuple-element.140, bf16[1,1024,2,512]{1,3,0,2:T(8,128)(2,1)S(1)} %get-tuple-element.139, bf16[2,4,1024,512,1]{3,2,0,1,4:T(8,128)(2,1)} %fusion.36), kind=kOutput, calls=%fused_computation.13 | convolution fusion | flops 8600420352 | bytes 16777216 | tf_op jit(solution)/shard_map/rfna,rnsj->jsfa/dot_general | solution.py:75
  764.7 80.1 %all-to-all-start = ((bf16[128,4,2,2048]{3,2,1,0:T(2,128)(2,1)}), bf16[128,4,2,2048]{3,2,1,0:T(2,128)(2,1)}, u32[]{:S(2)}, u32[]{:S(2)}) async-start(bf16[128,4,2,2048]{3,2,1,0:T(2,128)(2,1)} %constant_dynamic-update-slice_fusion.6), calls=%async_computation | async-start | bytes 8388608 | tf_op jit(solution)/shard_map/all_to_all | solution.py:14
  845.1 53.5 %all-to-all-done = bf16[128,4,2,2048]{3,2,1,0:T(2,128)(2,1)} async-done(((bf16[128,4,2,2048]{3,2,1,0:T(2,128)(2,1)}), bf16[128,4,2,2048]{3,2,1,0:T(2,128)(2,1)}, u32[]{:S(2)}, u32[]{:S(2)}) %all-to-all-start) | async-done | bytes 4194336 | tf_op jit(solution)/shard_map/all_to_all | solution.py:14
  898.5 7.6 reshape.427
  906.1 7.6 reshape.426
  913.8 3.6 fusion.24
  918.5 2.4 copy_negate_fusion
  921.0 4.4 copy.148
  925.4 2.4 maximum_bitcast_fusion.4
  927.8 20.7 %fusion = bf16[4,2,2,512,2,512]{3,5,2,4,1,0:T(8,128)(2,1)} fusion(bf16[4,1,2,64,2,4,512]{6,3,2,5,4,1,0:T(8,128)(2,1)} %maximum_bitcast_fusion.4, bf16[4,1,2,64,2,4,512]{6,3,2,5,4,1,0:T(8,128)(2,1)} %copy.148, bf16[4,2,64,2,4,512,1,1]{5,4,1,0,3,2,7,6:T(4,128)(2,1)} %bitcast.86), kind=kOutput, calls=%fused_computation.1 | convolution fusion | flops 8623489024 | bytes 29360128 | tf_op jit(solution)/shard_map/crtgfa,csrthfb->csgahb/dot_general | solution.py:84
  948.4 41.4 %copy.150 = bf16[4,2,2,512,2,512]{5,4,3,2,1,0:T(2,128)(2,1)} copy(bf16[4,2,2,512,2,512]{3,5,2,4,1,0:T(8,128)(2,1)} %fusion) | data formatting | bytes 33554432 | tf_op jit(solution)/shard_map/mul | solution.py:39
  989.8 27.4 %mul.287 = bf16[4,2,1024,1024]{3,2,1,0:T(8,128)(2,1)} reshape(bf16[4,2,2,512,2,512]{5,4,3,2,1,0:T(2,128)(2,1)} %copy.150) | data formatting | bytes 33554432 | tf_op jit(solution)/shard_map/mul | solution.py:39
  1017.3 9.3 fusion.2
  (524 shorter events, 271.7 us)
Async XLA Ops:
  7.3 412.9 %collective-permute-start.1 = (bf16[2,4,1024,512]{3,2,0,1:T(8,128)(2,1)}, bf16[2,4,1024,512]{3,2,0,1:T(8,128)(2,1)}, u32[]{:S(2)}, u32[]{:S(2)}) collective-permute-start(bf16[2,4,1024,512]{3,2,0,1:T(8,128)(2,1)} %copy.11), channel_id=1, source_target_pairs={{0,4},{2,6},{4,8},{6,10},{8,12},{10,14},{12,16},{14,18},{16,20},{1... | collective-permute-start | bytes 25165832 | tf_op jit(solution)/shard_map/ppermute | solution.py:21
  14.7 413.1 %collective-permute-start = (bf16[2,4,1024,512]{3,2,0,1:T(8,128)(2,1)}, bf16[2,4,1024,512]{3,2,0,1:T(8,128)(2,1)}, u32[]{:S(2)}, u32[]{:S(2)}) collective-permute-start(bf16[2,4,1024,512]{3,2,0,1:T(8,128)(2,1)} %copy.11), channel_id=1, source_target_pairs={{0,2},{2,4},{4,6},{6,8},{8,10},{10,12},{12,14},{14,16},{16,18},{18... | collective-permute-start | bytes 25165832 | tf_op jit(solution)/shard_map/ppermute | solution.py:21
  20.2 396.5 %collective-permute-start.2 = (bf16[2,3,1024,512]{3,2,0,1:T(8,128)(2,1)S(1)}, bf16[2,3,1024,512]{3,2,0,1:T(8,128)(2,1)}, u32[]{:S(2)}, u32[]{:S(2)}) collective-permute-start(bf16[2,3,1024,512]{3,2,0,1:T(8,128)(2,1)S(1)} %slice.257), channel_id=1, source_target_pairs={{0,6},{2,8},{4,10},{6,12},{8,14},{10,16},{12,18},{14,20},{16,22},{... | collective-permute-start | bytes 18874376 | tf_op jit(solution)/shard_map/ppermute | solution.py:21
  637.4 81.2 %copy-start.22 = (bf16[1,4,2,2048]{3,2,1,0:T(2,128)(2,1)S(1)}, bf16[1,4,2,2048]{3,2,1,0:T(2,128)(2,1)}, u32[]{:S(2)}) copy-start(bf16[1,4,2,2048]{3,2,1,0:T(2,128)(2,1)} %stack.482) | copy-start | bytes 98308
  637.4 81.8 %copy-start.23 = (bf16[1,4,2,2048]{3,2,1,0:T(2,128)(2,1)S(1)}, bf16[1,4,2,2048]{3,2,1,0:T(2,128)(2,1)}, u32[]{:S(2)}) copy-start(bf16[1,4,2,2048]{3,2,1,0:T(2,128)(2,1)} %stack.483) | copy-start | bytes 98308
  638.0 81.8 %copy-start.24 = (bf16[1,4,2,2048]{3,2,1,0:T(2,128)(2,1)S(1)}, bf16[1,4,2,2048]{3,2,1,0:T(2,128)(2,1)}, u32[]{:S(2)}) copy-start(bf16[1,4,2,2048]{3,2,1,0:T(2,128)(2,1)} %stack.484) | copy-start | bytes 98308
  638.0 82.5 %copy-start.25 = (bf16[1,4,2,2048]{3,2,1,0:T(2,128)(2,1)S(1)}, bf16[1,4,2,2048]{3,2,1,0:T(2,128)(2,1)}, u32[]{:S(2)}) copy-start(bf16[1,4,2,2048]{3,2,1,0:T(2,128)(2,1)} %stack.485) | copy-start | bytes 98308
  638.7 82.5 %copy-start.26 = (bf16[1,4,2,2048]{3,2,1,0:T(2,128)(2,1)S(1)}, bf16[1,4,2,2048]{3,2,1,0:T(2,128)(2,1)}, u32[]{:S(2)}) copy-start(bf16[1,4,2,2048]{3,2,1,0:T(2,128)(2,1)} %stack.486) | copy-start | bytes 98308
  638.7 83.1 %copy-start.27 = (bf16[1,4,2,2048]{3,2,1,0:T(2,128)(2,1)S(1)}, bf16[1,4,2,2048]{3,2,1,0:T(2,128)(2,1)}, u32[]{:S(2)}) copy-start(bf16[1,4,2,2048]{3,2,1,0:T(2,128)(2,1)} %stack.487) | copy-start | bytes 98308
  639.3 83.1 %copy-start.28 = (bf16[1,4,2,2048]{3,2,1,0:T(2,128)(2,1)S(1)}, bf16[1,4,2,2048]{3,2,1,0:T(2,128)(2,1)}, u32[]{:S(2)}) copy-start(bf16[1,4,2,2048]{3,2,1,0:T(2,128)(2,1)} %stack.488) | copy-start | bytes 98308
  639.3 83.7 %copy-start.29 = (bf16[1,4,2,2048]{3,2,1,0:T(2,128)(2,1)S(1)}, bf16[1,4,2,2048]{3,2,1,0:T(2,128)(2,1)}, u32[]{:S(2)}) copy-start(bf16[1,4,2,2048]{3,2,1,0:T(2,128)(2,1)} %stack.489) | copy-start | bytes 98308
  640.0 83.7 %copy-start.30 = (bf16[1,4,2,2048]{3,2,1,0:T(2,128)(2,1)S(1)}, bf16[1,4,2,2048]{3,2,1,0:T(2,128)(2,1)}, u32[]{:S(2)}) copy-start(bf16[1,4,2,2048]{3,2,1,0:T(2,128)(2,1)} %stack.490) | copy-start | bytes 98308
  640.0 84.4 %copy-start.31 = (bf16[1,4,2,2048]{3,2,1,0:T(2,128)(2,1)S(1)}, bf16[1,4,2,2048]{3,2,1,0:T(2,128)(2,1)}, u32[]{:S(2)}) copy-start(bf16[1,4,2,2048]{3,2,1,0:T(2,128)(2,1)} %stack.491) | copy-start | bytes 98308
  640.6 84.4 %copy-start.32 = (bf16[1,4,2,2048]{3,2,1,0:T(2,128)(2,1)S(1)}, bf16[1,4,2,2048]{3,2,1,0:T(2,128)(2,1)}, u32[]{:S(2)}) copy-start(bf16[1,4,2,2048]{3,2,1,0:T(2,128)(2,1)} %stack.492) | copy-start | bytes 98308
  640.6 85.0 %copy-start.33 = (bf16[1,4,2,2048]{3,2,1,0:T(2,128)(2,1)S(1)}, bf16[1,4,2,2048]{3,2,1,0:T(2,128)(2,1)}, u32[]{:S(2)}) copy-start(bf16[1,4,2,2048]{3,2,1,0:T(2,128)(2,1)} %stack.493) | copy-start | bytes 98308
  641.3 85.0 %copy-start.34 = (bf16[1,4,2,2048]{3,2,1,0:T(2,128)(2,1)S(1)}, bf16[1,4,2,2048]{3,2,1,0:T(2,128)(2,1)}, u32[]{:S(2)}) copy-start(bf16[1,4,2,2048]{3,2,1,0:T(2,128)(2,1)} %stack.494) | copy-start | bytes 98308
  641.3 85.6 %copy-start.35 = (bf16[1,4,2,2048]{3,2,1,0:T(2,128)(2,1)S(1)}, bf16[1,4,2,2048]{3,2,1,0:T(2,128)(2,1)}, u32[]{:S(2)}) copy-start(bf16[1,4,2,2048]{3,2,1,0:T(2,128)(2,1)} %stack.495) | copy-start | bytes 98308
  641.9 85.6 %copy-start.36 = (bf16[1,4,2,2048]{3,2,1,0:T(2,128)(2,1)S(1)}, bf16[1,4,2,2048]{3,2,1,0:T(2,128)(2,1)}, u32[]{:S(2)}) copy-start(bf16[1,4,2,2048]{3,2,1,0:T(2,128)(2,1)} %stack.496) | copy-start | bytes 98308
  641.9 86.3 %copy-start.37 = (bf16[1,4,2,2048]{3,2,1,0:T(2,128)(2,1)S(1)}, bf16[1,4,2,2048]{3,2,1,0:T(2,128)(2,1)}, u32[]{:S(2)}) copy-start(bf16[1,4,2,2048]{3,2,1,0:T(2,128)(2,1)} %stack.497) | copy-start | bytes 98308
  642.6 86.3 %copy-start.38 = (bf16[1,4,2,2048]{3,2,1,0:T(2,128)(2,1)S(1)}, bf16[1,4,2,2048]{3,2,1,0:T(2,128)(2,1)}, u32[]{:S(2)}) copy-start(bf16[1,4,2,2048]{3,2,1,0:T(2,128)(2,1)} %stack.498) | copy-start | bytes 98308
  643.2 86.3 %copy-start.39 = (bf16[1,4,2,2048]{3,2,1,0:T(2,128)(2,1)S(1)}, bf16[1,4,2,2048]{3,2,1,0:T(2,128)(2,1)}, u32[]{:S(2)}) copy-start(bf16[1,4,2,2048]{3,2,1,0:T(2,128)(2,1)} %stack.499) | copy-start | bytes 98308
  650.8 84.5 %copy-start.40 = (bf16[1,4,2,2048]{3,2,1,0:T(2,128)(2,1)S(1)}, bf16[1,4,2,2048]{3,2,1,0:T(2,128)(2,1)}, u32[]{:S(2)}) copy-start(bf16[1,4,2,2048]{3,2,1,0:T(2,128)(2,1)} %stack.508) | copy-start | bytes 98308
  651.4 84.5 %copy-start.41 = (bf16[1,4,2,2048]{3,2,1,0:T(2,128)(2,1)S(1)}, bf16[1,4,2,2048]{3,2,1,0:T(2,128)(2,1)}, u32[]{:S(2)}) copy-start(bf16[1,4,2,2048]{3,2,1,0:T(2,128)(2,1)} %stack.509) | copy-start | bytes 98308
  764.7 133.9 %all-to-all-start = ((bf16[128,4,2,2048]{3,2,1,0:T(2,128)(2,1)}), bf16[128,4,2,2048]{3,2,1,0:T(2,128)(2,1)}, u32[]{:S(2)}, u32[]{:S(2)}) async-start(bf16[128,4,2,2048]{3,2,1,0:T(2,128)(2,1)} %constant_dynamic-update-slice_fusion.6), calls=%async_computation | async-start | bytes 8388608 | tf_op jit(solution)/shard_map/all_to_all | solution.py:14
  (42 other events, 2505.5 us)
